TPU v7x, 128 devices: a whole 4x4x4 slice. The times are simulated.
128 devices in a mesh: member: 16 (over x_lo, y, core), lon: 8 (over x_hi, z).
Axes of the slice: x: 4 (x_hi: 2, x_lo: 2; x = x_hi * 2 + x_lo), y: 4, z: 4, core: 2. Of those that a mesh axis runs over, the one named last changes fastest.
Arguments:
- atmos: bfloat16 [16, 96, 96, 1024], P('member', None, None, 'lon'), may hold values from -6 to 6
- ocean: bfloat16 [96, 96, 1024], P(None, None, 'lon'), may hold values from -6 to 6
- land_mask: int32 [96, 1024], P(None, 'lon'), may hold values 0 or 1
- ice_mask: int32 [96, 1024], P(None, 'lon'), may hold values 0 or 1
- atm_kernel: float32 [2, 7, 7, 96], replicated, may hold values from -0.875 to 0.875
- atm_gain: float32 [2, 96], replicated, may hold values from 0.25 to 1.75
- atm_up: bfloat16 [2, 96, 384], replicated, may hold values from -0.625 to 0.625
- atm_down: bfloat16 [2, 384, 96], replicated, may hold values from -0.3125 to 0.3125
- atm_scale: float32 [2, 96], replicated, may hold values from 0.5 to 1.5
- flux_weight: bfloat16 [96, 32], replicated, may hold values from -0.625 to 0.625
- flux_lift: bfloat16 [2, 32, 96], replicated, may hold values from -1 to 1
- ocn_kernel: float32 [7, 7, 96], replicated, may hold values from -0.875 to 0.875
- ocn_gain: float32 [96], replicated, may hold values from 0.25 to 1.75
- ocn_up: bfloat16 [96, 384], replicated, may hold values from -0.625 to 0.625
- ocn_down: bfloat16 [384, 96], replicated, may hold values from -0.3125 to 0.3125
- ocn_scale: float32 [96], replicated, may hold values from 0.5 to 1.5
- surf_weight: bfloat16 [96, 8], replicated, may hold values from -0.625 to 0.625
- back_weight: bfloat16 [8, 96], replicated, may hold values from -2 to 2
Outputs:
- atmos_out: bfloat16 [16, 96, 96, 1024], P('member', None, None, 'lon')
- ocean_new: bfloat16 [96, 96, 1024], P('member', None, 'lon')
All inputs are finite; a program needn't handle non-finite values. No bound on the sum of `land_mask` or of `ice_mask` on one device may be relied on, other than what follows from the above.
Results may differ from a plain program's by a relative error of at most 0.017.
Values may be sent and summed in bfloat16 or wider, within the bound.
A program may use at most 64 MiB of HBM per device.

v0:
```python
import jax
import jax.numpy as jnp
from jax import lax
from jax.sharding import PartitionSpec as P


def with_halo(cells, sides, width):
    for axis, dim in sides:
        count = lax.axis_size(axis)
        head = lax.slice_in_dim(cells, 0, width, axis=dim)
        tail = lax.slice_in_dim(cells, cells.shape[dim] - width, cells.shape[dim], axis=dim)
        cells = jnp.concatenate(
            [
                lax.ppermute(tail, axis, [(i, (i + 1) % count) for i in range(count)]),
                cells,
                lax.ppermute(head, axis, [((i + 1) % count, i) for i in range(count)]),
            ],
            axis=dim,
        )
    return cells


def contract(form, left, right):
    return jnp.einsum(form, left.astype(jnp.float32), right.astype(jnp.float32))


def mixer(field, padded, kernel, gain, up_proj, down_proj, scale, keep):
    rows = field.shape[0]
    cols = field.shape[2]
    acc = jnp.zeros(field.shape, jnp.float32)
    for i in range(7):
        for j in range(7):
            acc = (
                acc
                + padded[i : i + rows, :, j : j + cols].astype(jnp.float32) * kernel[i, j][:, None]
            )
    center = acc - jnp.mean(acc, axis=1, keepdims=True)
    spread = jnp.mean(center * center, axis=1, keepdims=True)
    normed = (center * lax.rsqrt(spread + 1e-06) * gain[:, None]).astype(jnp.bfloat16)
    hidden = jax.nn.gelu(contract("lcw,ch->lhw", normed, up_proj)).astype(jnp.bfloat16)
    branch = contract("lhw,hc->lcw", hidden, down_proj)
    result = field.astype(jnp.float32) + scale[:, None] * branch
    if keep is not None:
        result = result * keep[:, None, :]
    return result.astype(jnp.bfloat16)


def atmos_pad(state):
    tall = jnp.pad(state, ((3, 3), (0, 0), (0, 0)))
    return with_halo(tall, (("lon", 2),), 3)


def forced(ocean_part, flux_sum, count, sea, ice, flux_lift):
    flux_low = (flux_sum / count).astype(jnp.bfloat16)
    open_term = contract("lfw,fc->lcw", flux_low, flux_lift[0])
    ice_term = contract("lfw,fc->lcw", flux_low, flux_lift[1])
    forcing = sea[:, None, :] * ((1.0 - ice)[:, None, :] * open_term + ice[:, None, :] * ice_term)
    return (ocean_part.astype(jnp.float32) + forcing).astype(jnp.bfloat16)


def local(
    atmos,
    ocean,
    land_mask,
    ice_mask,
    atm_kernel,
    atm_gain,
    atm_up,
    atm_down,
    atm_scale,
    flux_weight,
    flux_lift,
    ocn_kernel,
    ocn_gain,
    ocn_up,
    ocn_down,
    ocn_scale,
    surf_weight,
    back_weight,
):
    sea = (1 - land_mask).astype(jnp.float32)
    ice = ice_mask.astype(jnp.float32)
    state = atmos[0]
    for layer in range(2):
        state = mixer(
            state,
            atmos_pad(state),
            atm_kernel[layer],
            atm_gain[layer],
            atm_up[layer],
            atm_down[layer],
            atm_scale[layer],
            None,
        )
    flux = jax.nn.gelu(contract("lcw,cf->lfw", state, flux_weight))
    members = lax.axis_size("member")
    rank = lax.axis_index("member")
    rows = state.shape[0] // members
    flux_sum = lax.psum(flux.astype(jnp.bfloat16), "member").astype(jnp.float32)
    ocean_mid = forced(ocean, flux_sum, members, sea, ice, flux_lift)
    tall = jnp.pad(ocean_mid, ((3, 3), (0, 0), (0, 0)))
    padded = with_halo(tall, (("lon", 2),), 3)
    ocean_full = mixer(ocean_mid, padded, ocn_kernel, ocn_gain, ocn_up, ocn_down, ocn_scale, sea)
    surface = contract("lcw,cs->lsw", ocean_full, surf_weight).astype(jnp.bfloat16)
    ocean_rows = lax.dynamic_slice_in_dim(ocean_full, rank * rows, rows, 0)
    coupling = sea[:, None, :] * contract("lsw,sc->lcw", surface, back_weight)
    atmos_out = (state.astype(jnp.float32) + coupling).astype(jnp.bfloat16)[None]
    return (atmos_out, ocean_rows)


def solution(mesh):
    in_specs = (
        P("member", None, None, "lon"),
        P(None, None, "lon"),
        P(None, "lon"),
        P(None, "lon"),
        P(),
        P(),
        P(),
        P(),
        P(),
        P(),
        P(),
        P(),
        P(),
        P(),
        P(),
        P(),
        P(),
        P(),
    )
    out_specs = (P("member", None, None, "lon"), P("member", None, "lon"))
    return jax.shard_map(local, mesh=mesh, in_specs=in_specs, out_specs=out_specs, check_vma=False)
```

profile of v0, /device:TPU:1, one launch (start us, length us, event | category | flops | bytes accessed | tf_op | source)
XLA Modules:
  0.0 510.7 jit_solution(5957040996771305564)
XLA Ops:
  7.3 4.7 pad_slice_fusion.245
  11.9 3.3 copy.28
  20.0 4.8 collective-permute-start.1
  26.9 3.1 copy.29
  30.0 3.0 copy.32
  33.0 83.0 %fusion.313 = (f32[96,128]{1,0:T(8,128)S(1)}, f32[96,96,128]{2,1,0:T(8,128)}) fusion(f32[96]{0:T(128)S(1)} %get-tuple-element.115, bf16[102,96,3]{2,1,0:T(8,128)(2,1)} %copy.32, bf16[102,96,128]{2,1,0:T(8,128)(2,1)S(1)} %pad.10, f32[96]{0:T(128)S(1)} %get-tuple-element.116, f32[96]{0:T(128)S(1)} %get-tuple-element.117, f32[96]{0:T(128)S(1)} %get-tuple-element.118, ...), kind=kLoop, calls=%fused_computation.718 | loop fusion | flops 322031616 | bytes 23932160 | tf_op jit(solution)/shard_map/reduce_sum | solution.py:37
  116.0 3.6 multiply_reduce_fusion.2
  119.6 10.9 %fusion.61 = bf16[96,96,128]{2,1,0:T(8,128)(2,1)} fusion(f32[96]{0:T(128)S(1)} %get-tuple-element.169, f32[96,96,128]{2,1,0:T(8,128)} %get-tuple-element.7, f32[96]{0:T(128)S(1)} %get-tuple-element.164, f32[96,128]{1,0:T(8,128)S(1)} %add_rsqrt_fusion.2, f32[96,128]{1,0:T(8,128)S(1)} %broadcast_multiply_fusion.2, bf16[2,384,96]{1,2,0:T(8,128)(2,1)S(1)} %copy-done.16, ...), kind=kOutput, calls=%fused_computation.304 | convolution fusion | flops 1863843840 | bytes 9683968 | tf_op jit(solution)/shard_map/lhw,hc->lcw/dot_general | solution.py:24
  130.5 4.6 pad_slice_fusion.243
  135.2 3.3 copy.34
  140.8 5.1 %collective-permute-start.3 = (bf16[102,96,3]{0,1,2:T(8,128)(2,1)S(1)}, bf16[102,96,3]{0,1,2:T(8,128)(2,1)S(1)}, u32[]{:S(2)}, u32[]{:S(2)}) collective-permute-start(bf16[102,96,3]{0,1,2:T(8,128)(2,1)S(1)} %copy.37), channel_id=1, source_target_pairs={{1,0},{2,1},{3,2},{4,3},{5,4},{6,5},{7,6},{0,7},{9,8},{10,9},{11,1... | collective-permute-start | bytes 176264 | tf_op jit(solution)/shard_map/ppermute | solution.py:16
  147.8 3.5 copy.35
  154.3 82.9 %fusion.311 = (f32[96,128]{1,0:T(8,128)S(1)}, f32[96,96,128]{2,1,0:T(8,128)}) fusion(f32[96]{0:T(128)S(1)} %get-tuple-element.66, bf16[102,96,3]{2,1,0:T(8,128)(2,1)} %copy.38, bf16[102,96,128]{2,1,0:T(8,128)(2,1)S(1)} %pad.11, f32[96]{0:T(128)S(1)} %get-tuple-element.67, f32[96]{0:T(128)S(1)} %get-tuple-element.68, f32[96]{0:T(128)S(1)} %get-tuple-element.69, ...), kind=kLoop, calls=%fused_computation.717 | loop fusion | flops 322031616 | bytes 23932160 | tf_op jit(solution)/shard_map/reduce_sum | solution.py:37
  237.3 3.6 multiply_reduce_fusion.1
  240.9 10.9 %fusion.87 = bf16[96,96,128]{2,1,0:T(8,128)(2,1)} fusion(bf16[96,96,128]{2,1,0:T(8,128)(2,1)S(1)} %copy-done.4, f32[96]{0:T(128)S(1)} %get-tuple-element.170, f32[96,96,128]{2,1,0:T(8,128)} %get-tuple-element.5, f32[96]{0:T(128)S(1)} %get-tuple-element.163, f32[96,128]{1,0:T(8,128)S(1)} %add_rsqrt_fusion.1, f32[96,128]{1,0:T(8,128)S(1)} %broadcast_multiply_fusion.1, ...), kind=kOutput, calls=%fused_computation.330 | convolution fusion | flops 1863843840 | bytes 9683968 | tf_op jit(solution)/shard_map/lhw,hc->lcw/dot_general | solution.py:24
  251.8 3.4 fusion.267
  255.3 117.9 %all-reduce.5.cloned.1.call-done = bf16[96,32,128]{2,1,0:T(8,128)(2,1)} async-done(((bf16[96,32,128]{2,1,0:T(8,128)(2,1)}), bf16[96,32,128]{2,1,0:T(8,128)(2,1)}) %all-reduce.5.cloned.1.call-update) | async-done | bytes 786448 | tf_op jit(solution)/shard_map/psum | solution.py:99
  380.6 3.3 copy.40
  387.5 3.9 collective-permute-start.5
  393.2 3.3 copy.41
  399.6 82.9 %fusion.309 = (f32[96,128]{1,0:T(8,128)S(1)}, f32[96,96,128]{2,1,0:T(8,128)}) fusion(f32[96]{0:T(128)S(1)} %get-tuple-element.63, bf16[102,96,3]{2,1,0:T(8,128)(2,1)} %copy.43, bf16[102,96,128]{2,1,0:T(8,128)(2,1)S(1)} %pad.12, f32[96]{0:T(128)S(1)} %get-tuple-element.64, f32[96]{0:T(128)S(1)} %get-tuple-element.17, f32[96]{0:T(128)S(1)} %get-tuple-element.18, ...), kind=kLoop, calls=%fused_computation.716 | loop fusion | flops 322031616 | bytes 23932160 | tf_op jit(solution)/shard_map/reduce_sum | solution.py:37
  482.5 3.6 multiply_reduce_fusion
  486.2 11.0 %fusion.114 = bf16[96,96,128]{2,1,0:T(8,128)(2,1)} fusion(bf16[96,96,128]{2,1,0:T(8,128)(2,1)S(1)} %copy-done.2, f32[96,128]{1,0:T(8,128)S(1)} %subtract_convert_fusion, f32[96]{0:T(128)S(1)} %copy-done.20, f32[96,96,128]{2,1,0:T(8,128)} %get-tuple-element.3, f32[96]{0:T(128)S(1)} %copy-done.21, f32[96,128]{1,0:T(8,128)S(1)} %add_rsqrt_fusion, ...), kind=kOutput, calls=%fused_computation.357 | convolution fusion | flops 1865023488 | bytes 9732864 | tf_op jit(solution)/shard_map/lhw,hc->lcw/dot_general | solution.py:24
  498.8 4.8 fusion.117
  (88 shorter events, 31.6 us)
Async XLA Ops:
  7.2 478.9 %copy-start = (bf16[384,96]{0,1:T(8,128)(2,1)S(1)}, bf16[384,96]{0,1:T(8,128)(2,1)}, u32[]{:S(2)}) copy-start(bf16[384,96]{0,1:T(8,128)(2,1)} %param.32) | copy-start | bytes 221188
  7.2 366.0 %all-reduce.5.cloned.1.call-start = ((), (), s32[]{:S(2)}) async-start(), calls=%async_computation | async-start | bytes 1572864 | tf_op jit(solution)/shard_map/psum | solution.py:99
  7.2 17.6 %copy-start.8 = (f32[2,7,7,96]{3,0,2,1:T(2,128)S(1)}, f32[2,7,7,96]{3,0,2,1:T(2,128)}, u32[]{:S(2)}) copy-start(f32[2,7,7,96]{3,0,2,1:T(2,128)} %param.22) | copy-start | bytes 112900
  7.2 17.8 %copy-start.14 = (f32[2,96]{1,0:T(2,128)S(1)}, f32[2,96]{1,0:T(2,128)}, u32[]{:S(2)}) copy-start(f32[2,96]{1,0:T(2,128)} %param.23) | copy-start | bytes 2308
  7.2 17.8 %copy-start.15 = (f32[2,96]{1,0:T(2,128)S(1)}, f32[2,96]{1,0:T(2,128)}, u32[]{:S(2)}) copy-start(f32[2,96]{1,0:T(2,128)} %param.26) | copy-start | bytes 2308
  15.3 11.6 %collective-permute-start = (bf16[102,96,3]{0,1,2:T(8,128)(2,1)S(1)}, bf16[102,96,3]{0,1,2:T(8,128)(2,1)S(1)}, u32[]{:S(2)}, u32[]{:S(2)}) collective-permute-start(bf16[102,96,3]{0,1,2:T(8,128)(2,1)S(1)} %copy.28), channel_id=1, source_target_pairs={{0,1},{1,2},{2,3},{3,4},{4,5},{5,6},{6,7},{7,0},{8,9},{9,10},{10,1... | collective-permute-start | bytes 176264 | tf_op jit(solution)/shard_map/ppermute | solution.py:14
  20.0 10.0 %collective-permute-start.1 = (bf16[102,96,3]{0,1,2:T(8,128)(2,1)S(1)}, bf16[102,96,3]{0,1,2:T(8,128)(2,1)S(1)}, u32[]{:S(2)}, u32[]{:S(2)}) collective-permute-start(bf16[102,96,3]{0,1,2:T(8,128)(2,1)S(1)} %copy.31), channel_id=1, source_target_pairs={{1,0},{2,1},{3,2},{4,3},{5,4},{6,5},{7,6},{0,7},{9,8},{10,9},{11,1... | collective-permute-start | bytes 176264 | tf_op jit(solution)/shard_map/ppermute | solution.py:16
  116.0 3.6 copy-start.3
  116.0 3.6 copy-start.16
  116.0 3.6 copy-start.17
  138.5 9.3 %collective-permute-start.2 = (bf16[102,96,3]{0,1,2:T(8,128)(2,1)S(1)}, bf16[102,96,3]{0,1,2:T(8,128)(2,1)S(1)}, u32[]{:S(2)}, u32[]{:S(2)}) collective-permute-start(bf16[102,96,3]{0,1,2:T(8,128)(2,1)S(1)} %copy.34), channel_id=1, source_target_pairs={{0,1},{1,2},{2,3},{3,4},{4,5},{5,6},{6,7},{7,0},{8,9},{9,10},{10,1... | collective-permute-start | bytes 176264 | tf_op jit(solution)/shard_map/ppermute | solution.py:14
  140.8 10.4 %collective-permute-start.3 = (bf16[102,96,3]{0,1,2:T(8,128)(2,1)S(1)}, bf16[102,96,3]{0,1,2:T(8,128)(2,1)S(1)}, u32[]{:S(2)}, u32[]{:S(2)}) collective-permute-start(bf16[102,96,3]{0,1,2:T(8,128)(2,1)S(1)} %copy.37), channel_id=1, source_target_pairs={{1,0},{2,1},{3,2},{4,3},{5,4},{6,5},{7,6},{0,7},{9,8},{10,9},{11,1... | collective-permute-start | bytes 176264 | tf_op jit(solution)/shard_map/ppermute | solution.py:16
  237.2 3.6 copy-start.4
  240.9 10.9 %copy-start.19 = (bf16[96,32]{0,1:T(8,128)(2,1)S(1)}, bf16[96,32]{0,1:T(8,128)(2,1)}, u32[]{:S(2)}) copy-start(bf16[96,32]{0,1:T(8,128)(2,1)} %param.27) | copy-start | bytes 18436
  251.7 121.4 %copy-start.11 = (bf16[2,32,96]{2,1,0:T(8,128)(2,1)S(1)}, bf16[2,32,96]{2,1,0:T(8,128)(2,1)}, u32[]{:S(2)}) copy-start(bf16[2,32,96]{2,1,0:T(8,128)(2,1)} %param.28) | copy-start | bytes 36868
  251.8 123.4 %copy-start.6 = (bf16[96,96,128]{2,1,0:T(8,128)(2,1)S(1)}, bf16[96,96,128]{2,1,0:T(8,128)(2,1)}, u32[]{:S(2)}) copy-start(bf16[96,96,128]{2,1,0:T(8,128)(2,1)} %param.19) | copy-start | bytes 7077892
  383.9 9.3 %collective-permute-start.4 = (bf16[102,96,3]{0,1,2:T(8,128)(2,1)S(1)}, bf16[102,96,3]{0,1,2:T(8,128)(2,1)S(1)}, u32[]{:S(2)}, u32[]{:S(2)}) collective-permute-start(bf16[102,96,3]{0,1,2:T(8,128)(2,1)S(1)} %copy.40), channel_id=1, source_target_pairs={{0,1},{1,2},{2,3},{3,4},{4,5},{5,6},{6,7},{7,0},{8,9},{9,10},{10,1... | collective-permute-start | bytes 176264 | tf_op jit(solution)/shard_map/ppermute | solution.py:14
  387.5 9.0 %collective-permute-start.5 = (bf16[102,96,3]{0,1,2:T(8,128)(2,1)S(1)}, bf16[102,96,3]{0,1,2:T(8,128)(2,1)S(1)}, u32[]{:S(2)}, u32[]{:S(2)}) collective-permute-start(bf16[102,96,3]{0,1,2:T(8,128)(2,1)S(1)} %copy.42), channel_id=1, source_target_pairs={{1,0},{2,1},{3,2},{4,3},{5,4},{6,5},{7,6},{0,7},{9,8},{10,9},{11,1... | collective-permute-start | bytes 176264 | tf_op jit(solution)/shard_map/ppermute | solution.py:16
  482.4 3.7 copy-start.2
  482.5 3.7 copy-start.18
  482.5 3.7 copy-start.20
  482.5 3.7 copy-start.21
  486.1 12.6 %copy-start.12 = (bf16[8,96]{1,0:T(8,128)(2,1)S(1)}, bf16[8,96]{1,0:T(8,128)(2,1)}, u32[]{:S(2)}) copy-start(bf16[8,96]{1,0:T(8,128)(2,1)} %param.35) | copy-start | bytes 4612
  486.2 12.6 %copy-start.13 = (bf16[96,8]{0,1:T(8,128)(2,1)S(1)}, bf16[96,8]{0,1:T(8,128)(2,1)}, u32[]{:S(2)}) copy-start(bf16[96,8]{0,1:T(8,128)(2,1)} %param.34) | copy-start | bytes 4612
  (5 other events, 14.0 us)
Sparse Core Ops, SparseCore 0:
  255.3 117.8 all-reduce.4
where the time goes:
time: 514 us; the launch traced here: 511 us
  other arithmetic  260 us (51%)
  waiting for transfers between devices  118 us (23%)
  local copies, waits for them, and re-layouts  55.9 us (11%)
  matrix products  44.7 us (9%)
  starting transfers between devices  17.8 us (3%)
  between operations  14.9 us (3%)
    reduce_sum x3, other arithmetic, mixer(): center = acc - jnp.mean(acc, axis=1, keepdims=True)  249 us
    psum x1, waiting for transfers between devices, local(): flux_sum = lax.psum(flux.astype(jnp.bfloat16), 'member').astype(jnp.float32)  118 us
    dot_general x7, matrix products, contract(): return jnp.einsum(form, left.astype(jnp.float32), right.astype(jnp.float32))  44.7 us
    slice x6, local copies, waits for them, and re-layouts, with_halo(): lax.slice_in_dim(cells, cells.shape[dim] - width, cells.shape[dim], axis=...  21.6 us
    ppermute x3, starting transfers between devices, with_halo(): lax.ppermute(head, axis, [((i + 1) % count, i) for i in range(count)])  13.8 us
    reduce_sum x3, other arithmetic, mixer(): spread = jnp.mean(center * center, axis=1, keepdims=True)  10.7 us
  transfers between devices with their start and end apart: 7, of which 1 were waited for; matrix products, arithmetic and copies ran while one was open for 4% of the time, Pallas kernels for 0%

commit v1 on v0

--- a/solution.py
+++ b/solution.py
@@ -96,7 +96,9 @@
     members = lax.axis_size("member")
     rank = lax.axis_index("member")
     rows = state.shape[0] // members
-    flux_sum = lax.psum(flux.astype(jnp.bfloat16), "member").astype(jnp.float32)
+    flux_sum = jnp.sum(lax.all_gather(flux.astype(jnp.bfloat16), "member"), axis=0).astype(
+        jnp.float32
+    )
     ocean_mid = forced(ocean, flux_sum, members, sea, ice, flux_lift)
     tall = jnp.pad(ocean_mid, ((3, 3), (0, 0), (0, 0)))
     padded = with_halo(tall, (("lon", 2),), 3)

time: 514 us -> 477 us (0.928)
  waiting for transfers between devices: 118 us -> 71.7 us
  other arithmetic: 260 us -> 269 us
    psum x1 -> x0, waiting for transfers between devices: 118 us -> none  [local(): flux_sum = lax.psum(flux.astype(jnp.bfloat16), 'member').astype(jnp.float32)]
    all_gather x0 -> x1, waiting for transfers between devices: none -> 71.7 us  [local(): lax.all_gather(flux.astype(jnp.bfloat16), 'member')]
    reduce_sum x0 -> x1, other arithmetic: none -> 6.81 us  [local(): jnp.sum(lax.all_gather(flux.astype(jnp.bfloat16), 'member'), axis=0)]
  transfers between devices with their start and end apart: 7 -> 7, of which waited for: 1 -> 1; matrix products, arithmetic and copies ran while one was open for 4% -> 5% of each run, Pallas kernels for 0% -> 0%
where the time goes in v1:
time: 477 us; the launch traced here: 473 us
  other arithmetic  269 us (56%)
  waiting for transfers between devices  71.7 us (15%)
  local copies, waits for them, and re-layouts  56.5 us (12%)
  matrix products  43.4 us (9%)
  starting transfers between devices  17.9 us (4%)
  between operations  14.8 us (3%)
    reduce_sum x3, other arithmetic, mixer(): center = acc - jnp.mean(acc, axis=1, keepdims=True)  251 us
    all_gather x1, waiting for transfers between devices, local(): lax.all_gather(flux.astype(jnp.bfloat16), 'member')  71.7 us
    dot_general x7, matrix products, contract(): return jnp.einsum(form, left.astype(jnp.float32), right.astype(jnp.float32))  43.4 us
    slice x6, local copies, waits for them, and re-layouts, with_halo(): lax.slice_in_dim(cells, cells.shape[dim] - width, cells.shape[dim], axis=...  21.6 us
    ppermute x3, starting transfers between devices, with_halo(): lax.ppermute(head, axis, [((i + 1) % count, i) for i in range(count)])  13.9 us
    reduce_sum x3, other arithmetic, mixer(): spread = jnp.mean(center * center, axis=1, keepdims=True)  10.7 us
  transfers between devices with their start and end apart: 7, of which 1 were waited for; matrix products, arithmetic and copies ran while one was open for 5% of the time, Pallas kernels for 0%

profile of v1, /device:TPU:1, one launch (start us, length us, event | category | flops | bytes accessed | tf_op | source)
XLA Modules:
  0.0 473.1 jit_solution(7774750909527791697)
XLA Ops:
  7.3 4.7 pad_slice_fusion.245
  11.9 3.3 copy.28
  20.0 4.8 %collective-permute-start.1 = (bf16[102,96,3]{0,1,2:T(8,128)(2,1)S(1)}, bf16[102,96,3]{0,1,2:T(8,128)(2,1)S(1)}, u32[]{:S(2)}, u32[]{:S(2)}) collective-permute-start(bf16[102,96,3]{0,1,2:T(8,128)(2,1)S(1)} %copy.31), channel_id=1, source_target_pairs={{1,0},{2,1},{3,2},{4,3},{5,4},{6,5},{7,6},{0,7},{9,8},{10,9},{11,1... | collective-permute-start | bytes 176264 | tf_op jit(solution)/shard_map/ppermute | solution.py:16
  26.9 3.0 copy.29
  32.9 83.6 %fusion.313 = (f32[96,128]{1,0:T(8,128)S(1)}, f32[96,96,128]{2,1,0:T(8,128)}) fusion(f32[96]{0:T(128)S(1)} %get-tuple-element.115, bf16[102,96,3]{2,1,0:T(8,128)(2,1)} %copy.32, bf16[102,96,128]{2,1,0:T(8,128)(2,1)S(1)} %pad.10, f32[96]{0:T(128)S(1)} %get-tuple-element.116, f32[96]{0:T(128)S(1)} %get-tuple-element.117, f32[96]{0:T(128)S(1)} %get-tuple-element.118, ...), kind=kLoop, calls=%fused_computation.718 | loop fusion | flops 322031616 | bytes 23932160 | tf_op jit(solution)/shard_map/reduce_sum | solution.py:37
  116.6 3.6 multiply_reduce_fusion.2
  120.2 10.9 %fusion.61 = bf16[96,96,128]{2,1,0:T(8,128)(2,1)} fusion(f32[96]{0:T(128)S(1)} %get-tuple-element.169, f32[96,96,128]{2,1,0:T(8,128)} %get-tuple-element.7, f32[96]{0:T(128)S(1)} %get-tuple-element.164, f32[96,128]{1,0:T(8,128)S(1)} %add_rsqrt_fusion.2, f32[96,128]{1,0:T(8,128)S(1)} %broadcast_multiply_fusion.2, bf16[2,384,96]{1,2,0:T(8,128)(2,1)S(1)} %copy-done.15, ...), kind=kOutput, calls=%fused_computation.304 | convolution fusion | flops 1863843840 | bytes 9683968 | tf_op jit(solution)/shard_map/lhw,hc->lcw/dot_general | solution.py:24
  131.1 4.6 pad_slice_fusion.243
  135.8 3.3 copy.34
  141.4 5.1 %collective-permute-start.3 = (bf16[102,96,3]{0,1,2:T(8,128)(2,1)S(1)}, bf16[102,96,3]{0,1,2:T(8,128)(2,1)S(1)}, u32[]{:S(2)}, u32[]{:S(2)}) collective-permute-start(bf16[102,96,3]{0,1,2:T(8,128)(2,1)S(1)} %copy.37), channel_id=1, source_target_pairs={{1,0},{2,1},{3,2},{4,3},{5,4},{6,5},{7,6},{0,7},{9,8},{10,9},{11,1... | collective-permute-start | bytes 176264 | tf_op jit(solution)/shard_map/ppermute | solution.py:16
  148.4 3.4 copy.35
  154.8 83.7 %fusion.311 = (f32[96,128]{1,0:T(8,128)S(1)}, f32[96,96,128]{2,1,0:T(8,128)}) fusion(f32[96]{0:T(128)S(1)} %get-tuple-element.66, bf16[102,96,3]{2,1,0:T(8,128)(2,1)} %copy.38, bf16[102,96,128]{2,1,0:T(8,128)(2,1)S(1)} %pad.11, f32[96]{0:T(128)S(1)} %get-tuple-element.67, f32[96]{0:T(128)S(1)} %get-tuple-element.68, f32[96]{0:T(128)S(1)} %get-tuple-element.69, ...), kind=kLoop, calls=%fused_computation.717 | loop fusion | flops 322031616 | bytes 23932160 | tf_op jit(solution)/shard_map/reduce_sum | solution.py:37
  238.6 3.6 multiply_reduce_fusion.1
  242.2 10.9 %fusion.87 = bf16[96,96,128]{2,1,0:T(8,128)(2,1)} fusion(bf16[96,96,128]{2,1,0:T(8,128)(2,1)S(1)} %copy-done.4, f32[96]{0:T(128)S(1)} %get-tuple-element.170, f32[96,96,128]{2,1,0:T(8,128)} %get-tuple-element.5, f32[96]{0:T(128)S(1)} %get-tuple-element.163, f32[96,128]{1,0:T(8,128)S(1)} %add_rsqrt_fusion.1, f32[96,128]{1,0:T(8,128)S(1)} %broadcast_multiply_fusion.1, ...), kind=kOutput, calls=%fused_computation.330 | convolution fusion | flops 1863843840 | bytes 9683968 | tf_op jit(solution)/shard_map/lhw,hc->lcw/dot_general | solution.py:24
  253.1 3.3 fusion.267
  256.6 71.7 %all-gather.3.cloned.1.call-done = bf16[1536,32,128]{2,1,0:T(8,128)(2,1)} async-done(((bf16[96,32,128]{2,1,0:T(8,128)(2,1)}), bf16[1536,32,128]{2,1,0:T(8,128)(2,1)}) %all-gather.3.cloned.1.call-update) | async-done | bytes 12582928 | tf_op jit(solution)/shard_map/all_gather | solution.py:99
  328.3 6.8 %reduce_sum.70 = bf16[96,32,128]{2,1,0:T(8,128)(2,1)S(1)} reduce(bf16[16,96,32,128]{3,2,1,0:T(8,128)(2,1)} %bitcast.397, bf16[]{:T(256)} %constant.15.clone.1), dimensions={0}, to_apply=%region_4.5 | reduce | flops 5898240 | bytes 13369346 | tf_op jit(solution)/shard_map/reduce_sum | solution.py:99
  342.1 3.3 copy.40
  349.2 3.9 collective-permute-start.5
  355.0 3.0 copy.41
  361.0 83.8 %fusion.309 = (f32[96,128]{1,0:T(8,128)S(1)}, f32[96,96,128]{2,1,0:T(8,128)}) fusion(f32[96]{0:T(128)S(1)} %get-tuple-element.63, bf16[102,96,3]{2,1,0:T(8,128)(2,1)} %copy.43, bf16[102,96,128]{2,1,0:T(8,128)(2,1)S(1)} %pad.12, f32[96]{0:T(128)S(1)} %get-tuple-element.64, f32[96]{0:T(128)S(1)} %get-tuple-element.17, f32[96]{0:T(128)S(1)} %get-tuple-element.18, ...), kind=kLoop, calls=%fused_computation.716 | loop fusion | flops 322031616 | bytes 23932160 | tf_op jit(solution)/shard_map/reduce_sum | solution.py:37
  444.9 3.6 multiply_reduce_fusion
  448.5 11.0 %fusion.114 = bf16[96,96,128]{2,1,0:T(8,128)(2,1)} fusion(bf16[96,96,128]{2,1,0:T(8,128)(2,1)S(1)} %copy-done.2, f32[96,128]{1,0:T(8,128)S(1)} %subtract_convert_fusion, f32[96]{0:T(128)S(1)} %copy-done.19, f32[96,96,128]{2,1,0:T(8,128)} %get-tuple-element.3, f32[96]{0:T(128)S(1)} %copy-done.20, f32[96,128]{1,0:T(8,128)S(1)} %add_rsqrt_fusion, ...), kind=kOutput, calls=%fused_computation.357 | convolution fusion | flops 1865023488 | bytes 9732864 | tf_op jit(solution)/shard_map/lhw,hc->lcw/dot_general | solution.py:24
  461.2 4.8 %fusion.117 = bf16[1,96,96,128]{3,2,1,0:T(8,128)(2,1)} fusion(bf16[96,96,128]{2,1,0:T(8,128)(2,1)} %fusion.87, f32[96,128]{1,0:T(8,128)S(1)} %subtract_convert_fusion, bf16[96,96,128]{2,1,0:T(8,128)(2,1)} %fusion.114, bf16[8,96]{1,0:T(8,128)(2,1)S(1)} %copy-done.11, bf16[96,8]{0,1:T(8,128)(2,1)S(1)} %copy-done.12), kind=kOutput, calls=%fused_computation.369 | convolution fusion | flops 42565632 | bytes 7130112 | tf_op jit(solution)/shard_map/lsw,sc->lcw/dot_general | solution.py:24
  (87 shorter events, 34.4 us)
Async XLA Ops:
  7.2 441.3 %copy-start = (bf16[384,96]{0,1:T(8,128)(2,1)S(1)}, bf16[384,96]{0,1:T(8,128)(2,1)}, u32[]{:S(2)}) copy-start(bf16[384,96]{0,1:T(8,128)(2,1)} %param.32) | copy-start | bytes 221188
  7.2 321.1 %all-gather.3.cloned.1.call-start = ((), (), s32[]{:S(2)}) async-start(), calls=%async_computation | async-start | bytes 13369344 | tf_op jit(solution)/shard_map/all_gather | solution.py:99
  7.2 17.6 %copy-start.7 = (f32[2,7,7,96]{3,0,2,1:T(2,128)S(1)}, f32[2,7,7,96]{3,0,2,1:T(2,128)}, u32[]{:S(2)}) copy-start(f32[2,7,7,96]{3,0,2,1:T(2,128)} %param.22) | copy-start | bytes 112900
  7.2 17.8 %copy-start.13 = (f32[2,96]{1,0:T(2,128)S(1)}, f32[2,96]{1,0:T(2,128)}, u32[]{:S(2)}) copy-start(f32[2,96]{1,0:T(2,128)} %param.23) | copy-start | bytes 2308
  7.2 17.8 %copy-start.14 = (f32[2,96]{1,0:T(2,128)S(1)}, f32[2,96]{1,0:T(2,128)}, u32[]{:S(2)}) copy-start(f32[2,96]{1,0:T(2,128)} %param.26) | copy-start | bytes 2308
  15.3 11.6 %collective-permute-start = (bf16[102,96,3]{0,1,2:T(8,128)(2,1)S(1)}, bf16[102,96,3]{0,1,2:T(8,128)(2,1)S(1)}, u32[]{:S(2)}, u32[]{:S(2)}) collective-permute-start(bf16[102,96,3]{0,1,2:T(8,128)(2,1)S(1)} %copy.28), channel_id=1, source_target_pairs={{0,1},{1,2},{2,3},{3,4},{4,5},{5,6},{6,7},{7,0},{8,9},{9,10},{10,1... | collective-permute-start | bytes 176264 | tf_op jit(solution)/shard_map/ppermute | solution.py:14
  20.0 9.9 %collective-permute-start.1 = (bf16[102,96,3]{0,1,2:T(8,128)(2,1)S(1)}, bf16[102,96,3]{0,1,2:T(8,128)(2,1)S(1)}, u32[]{:S(2)}, u32[]{:S(2)}) collective-permute-start(bf16[102,96,3]{0,1,2:T(8,128)(2,1)S(1)} %copy.31), channel_id=1, source_target_pairs={{1,0},{2,1},{3,2},{4,3},{5,4},{6,5},{7,6},{0,7},{9,8},{10,9},{11,1... | collective-permute-start | bytes 176264 | tf_op jit(solution)/shard_map/ppermute | solution.py:16
  116.6 3.6 copy-start.3
  116.6 3.6 copy-start.15
  116.6 3.6 copy-start.16
  139.1 9.3 %collective-permute-start.2 = (bf16[102,96,3]{0,1,2:T(8,128)(2,1)S(1)}, bf16[102,96,3]{0,1,2:T(8,128)(2,1)S(1)}, u32[]{:S(2)}, u32[]{:S(2)}) collective-permute-start(bf16[102,96,3]{0,1,2:T(8,128)(2,1)S(1)} %copy.34), channel_id=1, source_target_pairs={{0,1},{1,2},{2,3},{3,4},{4,5},{5,6},{6,7},{7,0},{8,9},{9,10},{10,1... | collective-permute-start | bytes 176264 | tf_op jit(solution)/shard_map/ppermute | solution.py:14
  141.4 10.4 %collective-permute-start.3 = (bf16[102,96,3]{0,1,2:T(8,128)(2,1)S(1)}, bf16[102,96,3]{0,1,2:T(8,128)(2,1)S(1)}, u32[]{:S(2)}, u32[]{:S(2)}) collective-permute-start(bf16[102,96,3]{0,1,2:T(8,128)(2,1)S(1)} %copy.37), channel_id=1, source_target_pairs={{1,0},{2,1},{3,2},{4,3},{5,4},{6,5},{7,6},{0,7},{9,8},{10,9},{11,1... | collective-permute-start | bytes 176264 | tf_op jit(solution)/shard_map/ppermute | solution.py:16
  238.6 3.6 copy-start.4
  242.2 10.9 %copy-start.18 = (bf16[96,32]{0,1:T(8,128)(2,1)S(1)}, bf16[96,32]{0,1:T(8,128)(2,1)}, u32[]{:S(2)}) copy-start(bf16[96,32]{0,1:T(8,128)(2,1)} %param.27) | copy-start | bytes 18436
  253.1 3.5 copy-start.8
  328.3 6.8 %copy-start.10 = (bf16[2,32,96]{2,1,0:T(8,128)(2,1)S(1)}, bf16[2,32,96]{2,1,0:T(8,128)(2,1)}, u32[]{:S(2)}) copy-start(bf16[2,32,96]{2,1,0:T(8,128)(2,1)} %param.28) | copy-start | bytes 36868
  345.5 9.5 %collective-permute-start.4 = (bf16[102,96,3]{0,1,2:T(8,128)(2,1)S(1)}, bf16[102,96,3]{0,1,2:T(8,128)(2,1)S(1)}, u32[]{:S(2)}, u32[]{:S(2)}) collective-permute-start(bf16[102,96,3]{0,1,2:T(8,128)(2,1)S(1)} %copy.40), channel_id=1, source_target_pairs={{0,1},{1,2},{2,3},{3,4},{4,5},{5,6},{6,7},{7,0},{8,9},{9,10},{10,1... | collective-permute-start | bytes 176264 | tf_op jit(solution)/shard_map/ppermute | solution.py:14
  349.2 8.8 %collective-permute-start.5 = (bf16[102,96,3]{0,1,2:T(8,128)(2,1)S(1)}, bf16[102,96,3]{0,1,2:T(8,128)(2,1)S(1)}, u32[]{:S(2)}, u32[]{:S(2)}) collective-permute-start(bf16[102,96,3]{0,1,2:T(8,128)(2,1)S(1)} %copy.42), channel_id=1, source_target_pairs={{1,0},{2,1},{3,2},{4,3},{5,4},{6,5},{7,6},{0,7},{9,8},{10,9},{11,1... | collective-permute-start | bytes 176264 | tf_op jit(solution)/shard_map/ppermute | solution.py:16
  444.8 3.7 copy-start.2
  444.8 3.7 copy-start.17
  444.9 3.7 copy-start.19
  444.9 3.7 copy-start.20
  448.5 12.7 %copy-start.11 = (bf16[8,96]{1,0:T(8,128)(2,1)S(1)}, bf16[8,96]{1,0:T(8,128)(2,1)}, u32[]{:S(2)}) copy-start(bf16[8,96]{1,0:T(8,128)(2,1)} %param.35) | copy-start | bytes 4612
  448.5 12.6 %copy-start.12 = (bf16[96,8]{0,1:T(8,128)(2,1)S(1)}, bf16[96,8]{0,1:T(8,128)(2,1)}, u32[]{:S(2)}) copy-start(bf16[96,8]{0,1:T(8,128)(2,1)} %param.34) | copy-start | bytes 4612
  (4 other events, 9.8 us)
Sparse Core Ops, SparseCore 0:
  256.6 71.6 all-gather.2
